TPU v7x, 32 devices: a whole 2x2x4 slice. The times are simulated.
32 devices in a mesh: dp: 8 (over z, x), ctx: 4 (over y, core).
Axes of the slice: x: 2, y: 2, z: 4, core: 2. Of those that a mesh axis runs over, the one named last changes fastest.
Arguments:
- hidden: bfloat16 [8, 1024, 768], P('dp', 'ctx'), may hold values from -6 to 6
- teacher: bfloat16 [8, 1024, 768], P('dp', 'ctx'), may hold values from -12 to 12
- lengths: int32 [8], P('dp'), may hold values from 256 to 1024, as said below
- w_qkv: bfloat16 [768, 2304], P('dp'), may hold values from -0.21875 to 0.21875
- w_out: bfloat16 [768, 768], P('dp'), may hold values from -0.375 to 0.375
- w_up: bfloat16 [768, 3072], P('dp'), may hold values from -0.375 to 0.375
- w_down: bfloat16 [3072, 768], P('dp'), may hold values from -0.1875 to 0.1875
- norm_gain: bfloat16 [768, 3], P('dp'), may hold values from 0.099609375 to 1.8984375
- norm_shift: bfloat16 [768, 3], P('dp'), may hold values from -3 to 3
- proj_bias: bfloat16 [768, 4], P('dp'), may hold values from -3 to 3
- mid_gain: bfloat16 [3072], P('dp'), may hold values from 0.099609375 to 1.8984375
- mid_shift: bfloat16 [3072], P('dp'), may hold values from -3 to 3
- up_bias: bfloat16 [3072], P('dp'), may hold values from -3 to 3
Outputs:
- layer_output: bfloat16 [8, 1024, 768], P('dp', 'ctx')
- loss: float32 [], replicated
- hidden_grad: float32 [8, 1024, 768], P('dp', 'ctx')
- qkv_grad: float32 [768, 2304], P('dp')
- out_grad: float32 [768, 768], P('dp')
- up_grad: float32 [768, 3072], P('dp')
- down_grad: float32 [3072, 768], P('dp')
- gain_grad: float32 [768, 3], P('dp')
- shift_grad: float32 [768, 3], P('dp')
- bias_grad: float32 [768, 4], P('dp')
- mid_gain_grad: float32 [3072], P('dp')
- mid_shift_grad: float32 [3072], P('dp')
- up_bias_grad: float32 [3072], P('dp')
Inputs may be any that keep to these rules, and one draw needn't show every extreme that they name: Sequence s has valid tokens at positions 0 to lengths[s] - 1 and padding after them; some sequence has exactly 1024 and some exactly 256 valid tokens.
All inputs are finite; a program needn't handle non-finite values.
Results may differ from a plain program's by a relative error of at most 0.013.
Values may be sent and summed in bfloat16 or wider, within the bound.
No kernel may reach another device: no remote copies, remote signals or barrier semaphores. Data moves between devices by JAX's collectives and lax.ppermute only.
A program may use at most 192 MiB of HBM per device.

v0:
```python
import math
import jax
import jax.numpy as jnp
from jax import lax
from jax.sharding import PartitionSpec as P

HEADS = 12
HEAD_DIM = 64
EPSILON = 1e-05
NEGATIVE = -1e30


def passed_along(value, axis, steps):
    count = lax.axis_size(axis)
    pairs = [(source, (source + steps) % count) for source in range(count)]
    return lax.ppermute(value, axis, pairs)


def passed_along_2(block, axis, distance):
    devices = range(lax.axis_size(axis))
    route = [(i - distance, i) for i in devices if i - distance in devices]
    return lax.ppermute(block, axis, route)


def layer_norm(values, gain_vec, shift_vec):
    average = jnp.mean(values, axis=-1, keepdims=True)
    centred = values - average
    variance = jnp.mean(centred * centred, axis=-1, keepdims=True)
    return centred * lax.rsqrt(variance + EPSILON) * gain_vec + shift_vec


def mid_norm(up_proj, gain_vec, shift_vec):
    return layer_norm(jax.nn.gelu(up_proj, approximate=False), gain_vec, shift_vec)


def split_heads(values):
    return values.reshape(values.shape[0], values.shape[1], HEADS, HEAD_DIM)


def key_mask(query_pos, key_start, key_count, lengths):
    key_pos = key_start + jnp.arange(key_count, dtype=jnp.int32)
    causal = key_pos[None, :] <= query_pos[:, None]
    inside = key_pos[None, :] < lengths[:, None]
    return causal[None, :, :] & inside[:, None, :]


def fold_keys(running, pieces, key_start, heads_q, query_pos, lengths):
    row_max, row_total, weighted = running
    key_piece, value_piece = pieces
    key_count = key_piece.shape[1]
    score_scale = 1.0 / math.sqrt(HEAD_DIM)
    scores = (
        jnp.einsum(
            "sqhd,skhd->shqk", heads_q, split_heads(key_piece), preferred_element_type=jnp.float32
        )
        * score_scale
    )
    allowed = key_mask(query_pos, key_start, key_count, lengths)[:, None]
    scores = jnp.where(allowed, scores, NEGATIVE)
    fresh_max = jnp.maximum(row_max, jnp.max(scores, axis=-1))
    exponent_vals = jnp.exp(scores - fresh_max[..., None])
    row_total = jnp.sum(exponent_vals, axis=-1)
    update = jnp.einsum(
        "shqk,skhd->sqhd",
        exponent_vals.astype(jnp.bfloat16),
        split_heads(value_piece),
        preferred_element_type=jnp.float32,
    )
    weighted = update
    return (fresh_max, row_total, weighted)


def grad_keys(
    heads_q, heads_do, log_total, dterm, key_piece, value_piece, key_start, query_pos, lengths
):
    seq_count, key_count = (key_piece.shape[0], key_piece.shape[1])
    heads_k = split_heads(key_piece)
    heads_v = split_heads(value_piece)
    score_scale = 1.0 / math.sqrt(HEAD_DIM)
    scores = (
        jnp.einsum("sqhd,skhd->shqk", heads_q, heads_k, preferred_element_type=jnp.float32)
        * score_scale
    )
    allowed = key_mask(query_pos, key_start, key_count, lengths)[:, None]
    probability = jnp.where(allowed, jnp.exp(scores - log_total[..., None]), 0.0)
    dprob = jnp.einsum("sqhd,skhd->shqk", heads_do, heads_v, preferred_element_type=jnp.float32)
    dscores = (probability * (dprob - dterm[..., None])).astype(jnp.bfloat16)
    dq_part = (
        jnp.einsum("shqk,skhd->sqhd", dscores, heads_k, preferred_element_type=jnp.float32)
        * score_scale
    )
    dk_part = (
        jnp.einsum("shqk,sqhd->skhd", dscores, heads_q, preferred_element_type=jnp.float32)
        * score_scale
    )
    dv_part = jnp.einsum(
        "shqk,sqhd->skhd",
        probability.astype(jnp.bfloat16),
        heads_do,
        preferred_element_type=jnp.float32,
    )
    return (
        dq_part,
        dk_part.reshape(seq_count, key_count, -1),
        dv_part.reshape(seq_count, key_count, -1),
    )


def shards(
    hidden,
    teacher,
    lengths,
    w_qkv,
    w_out,
    w_up,
    w_down,
    norm_gain,
    norm_shift,
    proj_bias,
    mid_gain,
    mid_shift,
    up_bias,
):
    (
        full_qkv,
        full_out,
        full_up,
        full_down,
        gain_full,
        shift_full,
        bias_full,
        mid_gain_full,
        mid_shift_full,
        up_bias_full,
    ) = (
        lax.all_gather(w_qkv, "dp", axis=0, tiled=True),
        lax.all_gather(w_out, "dp", axis=0, tiled=True),
        lax.all_gather(w_up, "dp", axis=0, tiled=True),
        lax.all_gather(w_down, "dp", axis=0, tiled=True),
        lax.all_gather(norm_gain, "dp", axis=0, tiled=True),
        lax.all_gather(norm_shift, "dp", axis=0, tiled=True),
        lax.all_gather(proj_bias, "dp", axis=0, tiled=True),
        lax.all_gather(mid_gain, "dp", axis=0, tiled=True),
        lax.all_gather(mid_shift, "dp", axis=0, tiled=True),
        lax.all_gather(up_bias, "dp", axis=0, tiled=True),
    )
    gain_f = gain_full.astype(jnp.float32)
    shift_f = shift_full.astype(jnp.float32)
    bias_f = bias_full.astype(jnp.float32)
    mid_gain_f = mid_gain_full.astype(jnp.float32)
    mid_shift_f = mid_shift_full.astype(jnp.float32)
    up_bias_f = up_bias_full.astype(jnp.float32)
    seq_count, local_rows, model_width = hidden.shape
    token_rows = seq_count * local_rows
    seq_shape = (seq_count, local_rows, model_width)
    ctx_place = lax.axis_index("ctx")
    ctx_parts = lax.axis_size("ctx")
    query_pos = ctx_place * local_rows + jnp.arange(local_rows, dtype=jnp.int32)
    last_query = ctx_place * local_rows + local_rows - 1
    valid_mask = (query_pos[None, :] < lengths[:, None]).astype(jnp.float32)
    valid_rows = valid_mask.reshape(token_rows, 1)
    hidden_rows = hidden.reshape(token_rows, model_width).astype(jnp.float32)
    normed, pull_in = jax.vjp(layer_norm, hidden_rows, gain_f[:, 0], shift_f[:, 0])
    normed_low = normed.astype(jnp.bfloat16)
    projected = jnp.dot(normed_low, full_qkv, preferred_element_type=jnp.float32)
    query_low = (projected[:, :model_width] + bias_f[:, 0]).astype(jnp.bfloat16).reshape(seq_shape)
    key_low = projected[:, model_width : 2 * model_width].astype(jnp.bfloat16).reshape(seq_shape)
    value_low = (
        (projected[:, 2 * model_width :] + bias_f[:, 1]).astype(jnp.bfloat16).reshape(seq_shape)
    )
    heads_q = split_heads(query_low)
    start_state = (
        jnp.full((seq_count, HEADS, local_rows), NEGATIVE, jnp.float32),
        jnp.zeros((seq_count, HEADS, local_rows), jnp.float32),
        jnp.zeros((seq_count, local_rows, HEADS, HEAD_DIM), jnp.float32),
    )
    pieces = (
        lax.all_gather(key_low, "ctx", axis=1, tiled=True),
        lax.all_gather(value_low, "ctx", axis=1, tiled=True),
    )
    key_start = jnp.int32(0)
    row_max, row_total, weighted = lax.cond(
        key_start <= last_query,
        lambda: fold_keys(start_state, pieces, key_start, heads_q, query_pos, lengths),
        lambda: start_state,
    )
    attended = weighted / jnp.transpose(row_total, (0, 2, 1))[..., None]
    log_total = row_max + jnp.log(row_total)
    attended_rows = attended.reshape(token_rows, model_width)
    mixed, pull_mix = jax.vjp(layer_norm, attended_rows, gain_f[:, 1], shift_f[:, 1])
    mixed_low = mixed.astype(jnp.bfloat16)
    residual = (
        hidden_rows
        + jnp.dot(mixed_low, full_out, preferred_element_type=jnp.float32)
        + bias_f[:, 2]
    )
    ffn_in, pull_ffn = jax.vjp(layer_norm, residual, gain_f[:, 2], shift_f[:, 2])
    ffn_low = ffn_in.astype(jnp.bfloat16)
    up_proj = jnp.dot(ffn_low, full_up, preferred_element_type=jnp.float32) + up_bias_f
    activated, pull_mid = jax.vjp(mid_norm, up_proj, mid_gain_f, mid_shift_f)
    act_low = activated.astype(jnp.bfloat16)
    result = (
        residual + jnp.dot(act_low, full_down, preferred_element_type=jnp.float32) + bias_f[:, 3]
    )
    layer_output = (result * valid_rows).astype(jnp.bfloat16).reshape(hidden.shape)
    error_rows = (
        result - teacher.reshape(token_rows, model_width).astype(jnp.float32)
    ) * valid_rows
    loss_total, valid_total = lax.psum(
        (0.5 * jnp.sum(error_rows * error_rows), jnp.sum(valid_mask)), ("dp", "ctx")
    )
    loss = loss_total / (valid_total * model_width)
    down_low = error_rows.astype(jnp.bfloat16)
    bias_down_grad = jnp.sum(down_low.astype(jnp.float32), axis=0)
    down_grad = jnp.einsum("rf,rd->fd", act_low, down_low, preferred_element_type=jnp.float32)
    d_act = jnp.einsum("rd,fd->rf", down_low, full_down, preferred_element_type=jnp.float32)
    d_up, mid_gain_grad, mid_shift_grad = pull_mid(d_act)
    up_low = d_up.astype(jnp.bfloat16)
    up_bias_grad = jnp.sum(up_low.astype(jnp.float32), axis=0)
    up_grad = jnp.einsum("rd,rf->df", ffn_low, up_low, preferred_element_type=jnp.float32)
    d_ffn = jnp.einsum("rf,df->rd", up_low, full_up, preferred_element_type=jnp.float32)
    d_res_norm, gain_two, shift_two = pull_ffn(d_ffn)
    d_residual = error_rows + d_res_norm
    branch_low = d_residual.astype(jnp.bfloat16)
    bias_out_grad = jnp.sum(branch_low.astype(jnp.float32), axis=0)
    out_grad = jnp.einsum("rd,re->de", mixed_low, branch_low, preferred_element_type=jnp.float32)
    d_mixed = jnp.einsum("re,de->rd", branch_low, full_out, preferred_element_type=jnp.float32)
    d_att, gain_one, shift_one = pull_mix(d_mixed)
    heads_do = split_heads(d_att.astype(jnp.bfloat16).reshape(seq_shape))
    dterm = jnp.einsum("sqhd,sqhd->shq", heads_do.astype(jnp.float32), attended)

    def grad_step(key_piece, value_piece, key_start):
        return grad_keys(
            heads_q,
            heads_do,
            log_total,
            dterm,
            key_piece,
            value_piece,
            key_start,
            query_pos,
            lengths,
        )

    dq_zero = jnp.zeros((seq_count, local_rows, HEADS, HEAD_DIM), jnp.float32)
    own_zero = jnp.zeros(seq_shape, jnp.float32)

    def pass_step(step_index, running):
        key_cur, value_cur, dk_run, dv_run, dq_sum = running
        owner = (ctx_place - step_index) % ctx_parts
        dq_part, dk_part, dv_part = lax.cond(
            owner <= ctx_place,
            lambda: grad_step(key_cur, value_cur, owner * local_rows),
            lambda: (dq_zero, own_zero, own_zero),
        )
        dk_run, dv_run = (
            passed_along((dk_run + dk_part).astype(jnp.bfloat16), "ctx", 1).astype(jnp.float32),
            passed_along((dv_run + dv_part).astype(jnp.bfloat16), "ctx", 1).astype(jnp.float32),
        )
        key_cur, value_cur = passed_along_2((key_cur, value_cur), "ctx", 1)
        return (key_cur, value_cur, dk_run, dv_run, dq_sum + dq_part)

    key_end, value_end, dk_own, dv_own, dq_sum = lax.fori_loop(
        0, ctx_parts, pass_step, (key_low, value_low, own_zero, own_zero, dq_zero)
    )
    dq_low = dq_sum.reshape(token_rows, model_width).astype(jnp.bfloat16)
    dk_low = dk_own.reshape(token_rows, model_width).astype(jnp.bfloat16)
    dv_low = dv_own.reshape(token_rows, model_width).astype(jnp.bfloat16)
    dqkv_low = jnp.concatenate([dq_low, dk_low, dv_low], axis=1)
    bias_q_grad = jnp.sum(dq_low.astype(jnp.float32), axis=0)
    bias_v_grad = jnp.sum(dv_low.astype(jnp.float32), axis=0)
    qkv_grad = jnp.einsum("rd,re->de", normed_low, dqkv_low, preferred_element_type=jnp.float32)
    d_normed = jnp.einsum("re,de->rd", dqkv_low, full_qkv, preferred_element_type=jnp.float32)
    d_in_norm, gain_zero, shift_zero = pull_in(d_normed)
    hidden_grad = (d_residual + d_in_norm).reshape(hidden.shape)
    gain_grad = jnp.stack([gain_zero, gain_one, gain_two], axis=1)
    shift_grad = jnp.stack([shift_zero, shift_one, shift_two], axis=1)
    bias_grad = jnp.stack([bias_q_grad, bias_v_grad, bias_out_grad, bias_down_grad], axis=1)
    shares = (
        lax.psum_scatter(
            qkv_grad.astype(jnp.bfloat16), "dp", scatter_dimension=0, tiled=True
        ).astype(jnp.float32),
        lax.psum_scatter(
            out_grad.astype(jnp.bfloat16), "dp", scatter_dimension=0, tiled=True
        ).astype(jnp.float32),
        lax.psum_scatter(
            up_grad.astype(jnp.bfloat16), "dp", scatter_dimension=0, tiled=True
        ).astype(jnp.float32),
        lax.psum_scatter(
            down_grad.astype(jnp.bfloat16), "dp", scatter_dimension=0, tiled=True
        ).astype(jnp.float32),
        lax.psum_scatter(
            gain_grad.astype(jnp.bfloat16), "dp", scatter_dimension=0, tiled=True
        ).astype(jnp.float32),
        lax.psum_scatter(
            shift_grad.astype(jnp.bfloat16), "dp", scatter_dimension=0, tiled=True
        ).astype(jnp.float32),
        lax.psum_scatter(
            bias_grad.astype(jnp.bfloat16), "dp", scatter_dimension=0, tiled=True
        ).astype(jnp.float32),
        lax.psum_scatter(
            mid_gain_grad.astype(jnp.bfloat16), "dp", scatter_dimension=0, tiled=True
        ).astype(jnp.float32),
        lax.psum_scatter(
            mid_shift_grad.astype(jnp.bfloat16), "dp", scatter_dimension=0, tiled=True
        ).astype(jnp.float32),
        lax.psum_scatter(
            up_bias_grad.astype(jnp.bfloat16), "dp", scatter_dimension=0, tiled=True
        ).astype(jnp.float32),
    )
    summed = (
        lax.psum(shares[0].astype(jnp.bfloat16), "ctx").astype(jnp.float32),
        lax.psum(shares[1].astype(jnp.bfloat16), "ctx").astype(jnp.float32),
        lax.psum(shares[2].astype(jnp.bfloat16), "ctx").astype(jnp.float32),
        lax.psum(shares[3].astype(jnp.bfloat16), "ctx").astype(jnp.float32),
        lax.psum(shares[4].astype(jnp.bfloat16), "ctx").astype(jnp.float32),
        lax.psum(shares[5].astype(jnp.bfloat16), "ctx").astype(jnp.float32),
        lax.psum(shares[6].astype(jnp.bfloat16), "ctx").astype(jnp.float32),
        lax.psum(shares[7].astype(jnp.bfloat16), "ctx").astype(jnp.float32),
        lax.psum(shares[8].astype(jnp.bfloat16), "ctx").astype(jnp.float32),
        lax.psum(shares[9].astype(jnp.bfloat16), "ctx").astype(jnp.float32),
    )
    return (
        layer_output,
        loss,
        hidden_grad,
        summed[0],
        summed[1],
        summed[2],
        summed[3],
        summed[4],
        summed[5],
        summed[6],
        summed[7],
        summed[8],
        summed[9],
    )


def solution(mesh):
    placed = (
        P("dp", "ctx", None),
        P("dp", "ctx", None),
        P("dp"),
        P("dp", None),
        P("dp", None),
        P("dp", None),
        P("dp", None),
        P("dp", None),
        P("dp", None),
        P("dp", None),
        P("dp"),
        P("dp"),
        P("dp"),
    )
    return jax.shard_map(
        shards,
        mesh=mesh,
        in_specs=placed,
        out_specs=(
            P("dp", "ctx", None),
            P(),
            P("dp", "ctx", None),
            P("dp", None),
            P("dp", None),
            P("dp", None),
            P("dp", None),
            P("dp", None),
            P("dp", None),
            P("dp", None),
            P("dp"),
            P("dp"),
            P("dp"),
        ),
        check_vma=False,
    )
```

profile of v0, /device:TPU:0, one launch (start us, length us, event | category | flops | bytes accessed | tf_op | source)
XLA Modules:
  0.0 1042.5 jit_solution(1009641000833723574)
XLA Ops:
  8.0 22.6 %all-gather.3 = bf16[8,96,3]{1,2,0:T(4,128)(2,1)S(1)} all-gather(bf16[1,96,3]{1,2,0:T(4,128)(2,1)} %bitcast.185), channel_id=1, replica_groups=mesh['dp'=8,'ctx'=4] {'dp'}, dimensions={0}, use_global_device_ids=true | all-gather | bytes 5184 | tf_op jit(solution)/shard_map/all_gather | solution.py:141
  30.7 16.6 %all-gather.2 = bf16[8,96,3]{1,2,0:T(4,128)(2,1)S(1)} all-gather(bf16[1,96,3]{1,2,0:T(4,128)(2,1)} %bitcast.186), channel_id=1, replica_groups=mesh['dp'=8,'ctx'=4] {'dp'}, dimensions={0}, use_global_device_ids=true | all-gather | bytes 5184 | tf_op jit(solution)/shard_map/all_gather | solution.py:140
  49.9 28.3 %all-gather.15.cloned.1.call-done = bf16[768,2304]{1,0:T(8,128)(2,1)} async-done(((bf16[96,2304]{1,0:T(8,128)(2,1)}), bf16[768,2304]{1,0:T(8,128)(2,1)}) %all-gather.15.cloned.1.call-update) | async-done | bytes 3538960 | tf_op jit(solution)/shard_map/all_gather | solution.py:136
  78.2 3.3 fusion.73
  82.5 18.1 %all-gather.4 = bf16[8,96,4]{1,2,0:T(4,128)(2,1)S(1)} all-gather(bf16[1,96,4]{1,2,0:T(4,128)(2,1)S(1)} %bitcast.187), channel_id=1, replica_groups=mesh['dp'=8,'ctx'=4] {'dp'}, dimensions={0}, use_global_device_ids=true | all-gather | bytes 6912 | tf_op jit(solution)/shard_map/all_gather | solution.py:142
  104.1 25.9 %all-gather.5 = bf16[8,1,384]{2,1,0:T(2,128)(2,1)S(1)} all-gather(bf16[1,1,384]{2,1,0:T(2,128)(2,1)S(1)} %reshape.470), channel_id=1, replica_groups=mesh['dp'=8,'ctx'=4] {'dp'}, dimensions={0}, use_global_device_ids=true | all-gather | bytes 6912 | tf_op jit(solution)/shard_map/all_gather | solution.py:145
  130.0 26.1 %all-gather.7 = bf16[8,1,384]{2,1,0:T(2,128)(2,1)S(1)} all-gather(bf16[1,1,384]{2,1,0:T(2,128)(2,1)S(1)} %reshape.474), channel_id=1, replica_groups=mesh['dp'=8,'ctx'=4] {'dp'}, dimensions={0}, use_global_device_ids=true | all-gather | bytes 6912 | tf_op jit(solution)/shard_map/all_gather | solution.py:144
  156.1 26.1 %all-gather.6 = bf16[8,1,384]{2,1,0:T(2,128)(2,1)S(1)} all-gather(bf16[1,1,384]{2,1,0:T(2,128)(2,1)S(1)} %reshape.472), channel_id=1, replica_groups=mesh['dp'=8,'ctx'=4] {'dp'}, dimensions={0}, use_global_device_ids=true | all-gather | bytes 6912 | tf_op jit(solution)/shard_map/all_gather | solution.py:143
  185.1 21.4 %conditional.2 = (f32[1,12,256]{2,1,0:T(8,128)}, f32[1,12,256]{2,1,0:T(8,128)}, f32[1,256,12,64]{1,3,2,0:T(8,128)S(1)}, f32[1,12,256]{2,1,0:T(8,128)}) conditional(s32[]{:T(128)} %convert_element_type.247, () %tuple.48, (s32[256]{0:T(256)S(1)}, s32[1]{0:T(128)}, bf16[1,256,12,64]{1,3,2,0:T(8,128)(2,1)}, bf16[1,1024,768]{2,1,0:T(8,128)(2,1)}, ...), branch_computations={%region_2.0_spmd, %region_3.6_spmd} | conditional | flops 840431616 | bytes 106151000 | solution.py:182
  188.3 3.3 fusion.2
  192.3 4.1 fusion.4
  198.1 7.1 fusion.8
  211.1 35.4 %all-gather.19.cloned.1.call-done = bf16[768,3072]{1,0:T(8,128)(2,1)} async-done(((bf16[96,3072]{1,0:T(8,128)(2,1)}), bf16[768,3072]{1,0:T(8,128)(2,1)}) %all-gather.19.cloned.1.call-update) | async-done | bytes 4718608 | tf_op jit(solution)/shard_map/all_gather | solution.py:138
  246.5 12.0 %fusion.85 = (f32[256]{0:T(256)S(1)}, f32[256,3072]{1,0:T(8,128)S(1)}, f32[256,3072]{1,0:T(8,128)}, f32[256,3072]{1,0:T(8,128)}) fusion(f32[3072]{0:T(1024)S(1)} %bitcast.184, bf16[768,3072]{1,0:T(8,128)(2,1)} %all-gather.19.cloned.1.call-done, f32[256,768]{1,0:T(8,128)} %copy-done.6, f32[768]{0:T(1024)S(1)} %get-tuple-element.521, ...), kind=kOutput, calls=%fused_computation.178 | convolution fusion | flops 1260846848 | bytes 14963712 | tf_op jit(solution)/shard_map/dot_general | solution.py:199
  259.0 67.6 %all-gather.21.cloned.1.call-done = bf16[3072,768]{1,0:T(8,128)(2,1)} async-done(((bf16[384,768]{1,0:T(8,128)(2,1)}), bf16[3072,768]{1,0:T(8,128)(2,1)}) %all-gather.21.cloned.1.call-update) | async-done | bytes 4718608 | tf_op jit(solution)/shard_map/all_gather | solution.py:139
  326.6 5.8 convert_reduce_fusion.2
  337.5 3.2 fusion.78
  347.1 2.8 multiply_reduce_fusion.4
  354.7 144.0 %while.24 = (s32[]{:T(128)}, bf16[1,256,768]{1,2,0:T(8,128)(2,1)}, bf16[1,256,768]{1,2,0:T(8,128)(2,1)}, f32[1,256,768]{1,2,0:T(8,128)}, f32[1,256,768]{1,2,0:T(...) while((s32[]{:T(128)}, bf16[1,256,768]{1,2,0:T(8,128)(2,1)}, ...), condition=%wide.region_25.26_spmd.clone, body=%wide.region_22.25_spmd.clone.sunk | while | flops 513672192 | bytes 48655496 | solution.py:263
  358.2 14.6 %conditional.5 = (f32[1,256,12,64]{1,3,2,0:T(8,128)}, f32[1,256,768]{1,2,0:T(8,128)}, f32[1,256,768]{1,2,0:T(8,128)}) conditional(s32[]{:T(128)} %convert_element_type.407, () %tuple.115, (s32[]{:T(128)}, s32[]{:T(128)}, s32[1]{0:T(128)}, bf16[1,256,12,64]{1,3,2,0:T(8,128)(2,1)}, bf16[1,256,768]{1,2,0:T(8,128)(2,1)S(1)}, ...), branch_computations={%region_23.23_spmd, %region_24.24_spmd} | conditional | flops 511706112 | bytes 32138860 | solution.py:251
  358.2 3.3 fusion.28
  362.9 3.5 multiply_convert_fusion
  370.2 2.7 fusion.18
  378.4 2.7 collective-permute-start
  393.0 2.8 conditional.5
  398.0 16.3 %collective-permute-start.2 = (bf16[1,256,768]{1,2,0:T(8,128)(2,1)}, bf16[1,256,768]{1,2,0:T(8,128)(2,1)}, u32[]{:S(2)}, u32[]{:S(2)}) collective-permute-start(bf16[1,256,768]{1,2,0:T(8,128)(2,1)} %fusion.110), channel_id=1, source_target_pairs={{0,1},{1,2},{2,3},{3,0},{4,5},{5,6},{6,7},{7,4},{8,9},{9,10},{10,1... | collective-permute-start | bytes 1179656 | tf_op jit(solution)/shard_map/while/body/eval_jaxpr/ppermute | solution.py:16
  418.9 2.7 collective-permute-start
  433.2 2.8 conditional.5
  438.3 4.5 collective-permute-start.2
  445.0 14.2 %collective-permute-start.3 = (bf16[1,256,768]{1,2,0:T(8,128)(2,1)}, bf16[1,256,768]{1,2,0:T(8,128)(2,1)}, u32[]{:S(2)}, u32[]{:S(2)}) collective-permute-start(bf16[1,256,768]{1,2,0:T(8,128)(2,1)} %fusion.111), channel_id=1, source_target_pairs={{0,1},{1,2},{2,3},{3,0},{4,5},{5,6},{6,7},{7,4},{8,9},{9,10},{10,1... | collective-permute-start | bytes 1179656 | tf_op jit(solution)/shard_map/while/body/eval_jaxpr/ppermute | solution.py:16
  459.2 2.7 collective-permute-start
  473.5 2.8 conditional.5
  478.5 4.5 collective-permute-start.2
  487.7 2.7 collective-permute-start
  504.1 3.1 convolution_convert_fusion.2
  507.3 5.4 convolution_convert_fusion.1
  513.3 5.1 convolution_convert_fusion
  519.7 3.9 fusion.77
  541.5 48.6 %reduce-scatter.14.cloned.1.call-done = bf16[96,2304]{1,0:T(8,128)(2,1)} async-done(((bf16[768,2304]{1,0:T(8,128)(2,1)}), bf16[96,2304]{1,0:T(8,128)(2,1)}) %reduce-scatter.14.cloned.1.call-update) | async-done | bytes 442384 | tf_op jit(solution)/shard_map/reduce_scatter | solution.py:280
  590.1 98.8 %reduce-scatter.18.cloned.1.call-done = bf16[96,3072]{1,0:T(8,128)(2,1)} async-done(((bf16[768,3072]{1,0:T(8,128)(2,1)}), bf16[96,3072]{1,0:T(8,128)(2,1)}) %reduce-scatter.18.cloned.1.call-update) | async-done | bytes 589840 | tf_op jit(solution)/shard_map/reduce_scatter | solution.py:286
  689.0 98.5 %reduce-scatter.20.cloned.1.call-done = bf16[384,768]{1,0:T(8,128)(2,1)} async-done(((bf16[3072,768]{1,0:T(8,128)(2,1)}), bf16[384,768]{1,0:T(8,128)(2,1)}) %reduce-scatter.20.cloned.1.call-update) | async-done | bytes 589840 | tf_op jit(solution)/shard_map/reduce_scatter | solution.py:289
  790.1 2.6 add_bitcast_fusion
  793.9 40.5 %all-reduce.3 = (f32[]{:T(128)}, f32[]{:T(128)}) all-reduce(f32[]{:T(128)S(6)} %mul.346, f32[]{:T(128)} %fusion.71), channel_id=1, replica_groups=mesh['dp'=8,'ctx'=4] {'dp','ctx'}, use_global_device_ids=true, to_apply=%region_13.14 | all-reduce | flops 2 | bytes 16 | tf_op jit(solution)/shard_map/psum | solution.py:209
  834.5 36.7 %all-reduce.4 = (bf16[3072]{0:T(1024)(128)(2,1)S(1)}, bf16[3072]{0:T(1024)(128)(2,1)S(1)}, bf16[3072]{0:T(1024)(128)(2,1)S(1)}) all-reduce(bf16[3072]{0:T(1024)(128)(2,1)} %get-tuple-element.504, bf16[3072]{0:T(1024)(128)(2,1)} %get-tuple-element.506, bf16[3072]{0:T(1024)(128)(2,1)S(1)} %copy-done.41), channel_id=11, replica_groups=mesh['dp'=8,'ctx'=4] {'dp'}, use_global_device_ids=true, to_apply=%region_53.54.clone | all-reduce | flops 9216 | bytes 36864
  875.0 41.1 %reduce-scatter.24.cloned.1.call-done = bf16[96,3]{1,0:T(8,128)(2,1)} async-done(((bf16[768,3]{1,0:T(8,128)(2,1)}), bf16[96,3]{1,0:T(8,128)(2,1)}) %reduce-scatter.24.cloned.1.call-update) | async-done | bytes 592
  916.9 62.6 %reduce-scatter.26.cloned.1.call-done = bf16[96,4]{1,0:T(8,128)(2,1)} async-done(((bf16[768,4]{1,0:T(8,128)(2,1)}), bf16[96,4]{1,0:T(8,128)(2,1)}) %reduce-scatter.26.cloned.1.call-update) | async-done | bytes 784
  980.3 5.7 all-reduce.5
  989.5 38.1 %all-reduce.9.cloned.1.call-done = (bf16[96,2304]{1,0:T(8,128)(2,1)}, bf16[96,768]{1,0:T(8,128)(2,1)}, bf16[96,3072]{1,0:T(8,128)(2,1)}, bf16[384,768]{1,0:T(8,128)(2,1)}) async-done(((bf16[96,2304]{1,0:T(8,128)(2,1)}, bf16[96,768]{1,0:T(8,128)(2,1)}, bf16[96,3072]{1,0:T(8,128)(2,1)}, bf16[384,768]{1,0:T(8,128)(2,1)}), (bf16[96,2304]{1,0:T(8,128)(2,1)}, bf16[96,768]{1,0:T(8,128)(2,1)}, ...) | async-done | bytes 1769488 | tf_op jit(solution)/shard_map/psum | solution.py:312
  (360 shorter events, 164.0 us)
Async XLA Ops:
  7.2 71.0 %all-gather.15.cloned.1.call-start = ((), (), s32[]{:S(2)}) async-start(), calls=%async_computation.7 | async-start | bytes 3981312 | tf_op jit(solution)/shard_map/all_gather | solution.py:136
  7.9 177.2 %all-gather.23.cloned.1.call-start = ((), (), s32[]{:S(2)}) async-start(), calls=%async_computation.15 | async-start | bytes 1966080 | tf_op jit(solution)/shard_map/all_gather | solution.py:178
  47.4 160.5 %copy-start.33 = (f32[768]{0:T(1024)}, f32[768]{0:T(1024)S(1)}, u32[]{:S(2)}) copy-start(f32[768]{0:T(1024)S(1)} %get-tuple-element.605) | copy-start | bytes 9220
  47.4 160.5 %copy-start.48 = (f32[768]{0:T(1024)}, f32[768]{0:T(1024)S(1)}, u32[]{:S(2)}) copy-start(f32[768]{0:T(1024)S(1)} %get-tuple-element.522) | copy-start | bytes 9220
  47.4 199.0 %copy-start.32 = (f32[768]{0:T(1024)}, f32[768]{0:T(1024)S(1)}, u32[]{:S(2)}) copy-start(f32[768]{0:T(1024)S(1)} %get-tuple-element.521) | copy-start | bytes 9220
  81.6 48.4 %copy-start.71 = (bf16[384]{0:T(512)(128)(2,1)S(1)}, bf16[384]{0:T(512)(128)(2,1)}, u32[]{:S(2)}) copy-start(bf16[384]{0:T(512)(128)(2,1)} %param.30) | copy-start | bytes 2308
  81.6 74.5 %copy-start.72 = (bf16[384]{0:T(512)(128)(2,1)S(1)}, bf16[384]{0:T(512)(128)(2,1)}, u32[]{:S(2)}) copy-start(bf16[384]{0:T(512)(128)(2,1)} %param.29) | copy-start | bytes 2308
  82.4 102.7 %all-gather.25.cloned.1.call-start = ((), (), s32[]{:S(2)}) async-start(), calls=%async_computation.16 | async-start | bytes 1966080 | tf_op jit(solution)/shard_map/all_gather | solution.py:179
  101.6 82.7 %copy-start.17 = (bf16[256,768]{1,0:T(8,128)(2,1)S(1)}, bf16[256,768]{1,0:T(8,128)(2,1)}, u32[]{:S(2)}) copy-start(bf16[256,768]{1,0:T(8,128)(2,1)} %get-tuple-element.592) | copy-start | bytes 1179652
  101.6 106.4 %all-gather.17.cloned.1.call-start = ((), (), s32[]{:S(2)}) async-start(), calls=%async_computation.8 | async-start | bytes 1327104 | tf_op jit(solution)/shard_map/all_gather | solution.py:137
  102.2 144.3 %all-gather.19.cloned.1.call-start = ((), (), s32[]{:S(2)}) async-start(), calls=%async_computation.9 | async-start | bytes 5308416 | tf_op jit(solution)/shard_map/all_gather | solution.py:138
  102.7 223.8 %all-gather.21.cloned.1.call-start = ((), (), s32[]{:S(2)}) async-start(), calls=%async_computation.10 | async-start | bytes 5308416 | tf_op jit(solution)/shard_map/all_gather | solution.py:139
  103.3 438.2 %reduce-scatter.16.cloned.1.call-start = ((), (), s32[]{:S(2)}) async-start(), calls=%async_computation.12 | async-start | bytes 1327104 | tf_op jit(solution)/shard_map/reduce_scatter | solution.py:283
  156.1 170.4 %copy-start.29 = (f32[8,1,384]{2,1,0:T(1,128)}, f32[8,1,384]{2,1,0:T(1,128)S(1)}, u32[]{:S(2)}) copy-start(f32[8,1,384]{2,1,0:T(1,128)S(1)} %convert_element_type.300) | copy-start | bytes 36868
  182.3 144.3 %copy-start.66 = (f32[256]{0:T(256)}, f32[256]{0:T(256)S(1)}, u32[]{:S(2)}) copy-start(f32[256]{0:T(256)S(1)} %compare_convert_fusion) | copy-start | bytes 3076
  207.7 38.7 %copy-start.10 = (f32[256,768]{1,0:T(8,128)}, f32[256,768]{1,0:T(8,128)S(1)}, u32[]{:S(2)}) copy-start(f32[256,768]{1,0:T(8,128)S(1)} %copy.62) | copy-start | bytes 2359300
  207.8 50.7 %copy-start.45 = (f32[256]{0:T(256)}, f32[256]{0:T(256)S(1)}, u32[]{:S(2)}) copy-start(f32[256]{0:T(256)S(1)} %broadcast_multiply_fusion.2) | copy-start | bytes 3076
  210.0 134.1 %copy-start.40 = (f32[256]{0:T(256)}, f32[256]{0:T(256)S(1)}, u32[]{:S(2)}) copy-start(f32[256]{0:T(256)S(1)} %broadcast_multiply_fusion.1) | copy-start | bytes 3076
  211.1 133.0 %copy-start.51 = (f32[256]{0:T(256)}, f32[256]{0:T(256)S(1)}, u32[]{:S(2)}) copy-start(f32[256]{0:T(256)S(1)} %fusion.64) | copy-start | bytes 3076
  258.5 78.1 %copy-start.30 = (f32[256]{0:T(256)}, f32[256]{0:T(256)S(1)}, u32[]{:S(2)}) copy-start(f32[256]{0:T(256)S(1)} %broadcast_multiply_fusion) | copy-start | bytes 3076
  258.9 77.6 %copy-start.39 = (f32[256]{0:T(256)}, f32[256]{0:T(256)S(1)}, u32[]{:S(2)}) copy-start(f32[256]{0:T(256)S(1)} %fusion.65) | copy-start | bytes 3076
  353.3 236.9 %reduce-scatter.14.cloned.1.call-start = ((), (), s32[]{:S(2)}) async-start(), calls=%async_computation.11 | async-start | bytes 3981312 | tf_op jit(solution)/shard_map/reduce_scatter | solution.py:280
  374.8 11.0 %collective-permute-start.2 = (bf16[1,256,768]{1,2,0:T(8,128)(2,1)}, bf16[1,256,768]{1,2,0:T(8,128)(2,1)}, u32[]{:S(2)}, u32[]{:S(2)}) collective-permute-start(bf16[1,256,768]{1,2,0:T(8,128)(2,1)} %fusion.110), channel_id=1, source_target_pairs={{0,1},{1,2},{2,3},{3,0},{4,5},{5,6},{6,7},{7,4},{8,9},{9,10},{10,1... | collective-permute-start | bytes 1179656 | tf_op jit(solution)/shard_map/while/body/eval_jaxpr/ppermute | solution.py:16
  376.8 10.9 %collective-permute-start.3 = (bf16[1,256,768]{1,2,0:T(8,128)(2,1)}, bf16[1,256,768]{1,2,0:T(8,128)(2,1)}, u32[]{:S(2)}, u32[]{:S(2)}) collective-permute-start(bf16[1,256,768]{1,2,0:T(8,128)(2,1)} %fusion.111), channel_id=1, source_target_pairs={{0,1},{1,2},{2,3},{3,0},{4,5},{5,6},{6,7},{7,4},{8,9},{9,10},{10,1... | collective-permute-start | bytes 1179656 | tf_op jit(solution)/shard_map/while/body/eval_jaxpr/ppermute | solution.py:16
  378.4 11.2 %collective-permute-start = (bf16[1,256,768]{1,2,0:T(8,128)(2,1)S(1)}, bf16[1,256,768]{1,2,0:T(8,128)(2,1)}, u32[]{:S(2)}, u32[]{:S(2)}) collective-permute-start(bf16[1,256,768]{1,2,0:T(8,128)(2,1)S(1)} %copy.106), channel_id=1, source_target_pairs={{0,1},{1,2},{2,3},{4,5},{5,6},{6,7},{8,9},{9,10},{10,11},{12,13},{... | collective-permute-start | bytes 1179656 | tf_op jit(solution)/shard_map/while/body/eval_jaxpr/ppermute | solution.py:22
  381.1 8.5 collective-permute-start.1
  398.0 28.0 %collective-permute-start.2 = (bf16[1,256,768]{1,2,0:T(8,128)(2,1)}, bf16[1,256,768]{1,2,0:T(8,128)(2,1)}, u32[]{:S(2)}, u32[]{:S(2)}) collective-permute-start(bf16[1,256,768]{1,2,0:T(8,128)(2,1)} %fusion.110), channel_id=1, source_target_pairs={{0,1},{1,2},{2,3},{3,0},{4,5},{5,6},{6,7},{7,4},{8,9},{9,10},{10,1... | collective-permute-start | bytes 1179656 | tf_op jit(solution)/shard_map/while/body/eval_jaxpr/ppermute | solution.py:16
  416.6 11.4 %collective-permute-start.3 = (bf16[1,256,768]{1,2,0:T(8,128)(2,1)}, bf16[1,256,768]{1,2,0:T(8,128)(2,1)}, u32[]{:S(2)}, u32[]{:S(2)}) collective-permute-start(bf16[1,256,768]{1,2,0:T(8,128)(2,1)} %fusion.111), channel_id=1, source_target_pairs={{0,1},{1,2},{2,3},{3,0},{4,5},{5,6},{6,7},{7,4},{8,9},{9,10},{10,1... | collective-permute-start | bytes 1179656 | tf_op jit(solution)/shard_map/while/body/eval_jaxpr/ppermute | solution.py:16
  418.9 11.0 %collective-permute-start = (bf16[1,256,768]{1,2,0:T(8,128)(2,1)S(1)}, bf16[1,256,768]{1,2,0:T(8,128)(2,1)}, u32[]{:S(2)}, u32[]{:S(2)}) collective-permute-start(bf16[1,256,768]{1,2,0:T(8,128)(2,1)S(1)} %copy.106), channel_id=1, source_target_pairs={{0,1},{1,2},{2,3},{4,5},{5,6},{6,7},{8,9},{9,10},{10,11},{12,13},{... | collective-permute-start | bytes 1179656 | tf_op jit(solution)/shard_map/while/body/eval_jaxpr/ppermute | solution.py:22
  421.6 8.3 collective-permute-start.1
  438.3 28.0 %collective-permute-start.2 = (bf16[1,256,768]{1,2,0:T(8,128)(2,1)}, bf16[1,256,768]{1,2,0:T(8,128)(2,1)}, u32[]{:S(2)}, u32[]{:S(2)}) collective-permute-start(bf16[1,256,768]{1,2,0:T(8,128)(2,1)} %fusion.110), channel_id=1, source_target_pairs={{0,1},{1,2},{2,3},{3,0},{4,5},{5,6},{6,7},{7,4},{8,9},{9,10},{10,1... | collective-permute-start | bytes 1179656 | tf_op jit(solution)/shard_map/while/body/eval_jaxpr/ppermute | solution.py:16
  445.0 23.2 %collective-permute-start.3 = (bf16[1,256,768]{1,2,0:T(8,128)(2,1)}, bf16[1,256,768]{1,2,0:T(8,128)(2,1)}, u32[]{:S(2)}, u32[]{:S(2)}) collective-permute-start(bf16[1,256,768]{1,2,0:T(8,128)(2,1)} %fusion.111), channel_id=1, source_target_pairs={{0,1},{1,2},{2,3},{3,0},{4,5},{5,6},{6,7},{7,4},{8,9},{9,10},{10,1... | collective-permute-start | bytes 1179656 | tf_op jit(solution)/shard_map/while/body/eval_jaxpr/ppermute | solution.py:16
  459.2 10.9 %collective-permute-start = (bf16[1,256,768]{1,2,0:T(8,128)(2,1)S(1)}, bf16[1,256,768]{1,2,0:T(8,128)(2,1)}, u32[]{:S(2)}, u32[]{:S(2)}) collective-permute-start(bf16[1,256,768]{1,2,0:T(8,128)(2,1)S(1)} %copy.106), channel_id=1, source_target_pairs={{0,1},{1,2},{2,3},{4,5},{5,6},{6,7},{8,9},{9,10},{10,11},{12,13},{... | collective-permute-start | bytes 1179656 | tf_op jit(solution)/shard_map/while/body/eval_jaxpr/ppermute | solution.py:22
  461.9 8.3 collective-permute-start.1
  478.5 16.3 %collective-permute-start.2 = (bf16[1,256,768]{1,2,0:T(8,128)(2,1)}, bf16[1,256,768]{1,2,0:T(8,128)(2,1)}, u32[]{:S(2)}, u32[]{:S(2)}) collective-permute-start(bf16[1,256,768]{1,2,0:T(8,128)(2,1)} %fusion.110), channel_id=1, source_target_pairs={{0,1},{1,2},{2,3},{3,0},{4,5},{5,6},{6,7},{7,4},{8,9},{9,10},{10,1... | collective-permute-start | bytes 1179656 | tf_op jit(solution)/shard_map/while/body/eval_jaxpr/ppermute | solution.py:16
  485.2 11.5 %collective-permute-start.3 = (bf16[1,256,768]{1,2,0:T(8,128)(2,1)}, bf16[1,256,768]{1,2,0:T(8,128)(2,1)}, u32[]{:S(2)}, u32[]{:S(2)}) collective-permute-start(bf16[1,256,768]{1,2,0:T(8,128)(2,1)} %fusion.111), channel_id=1, source_target_pairs={{0,1},{1,2},{2,3},{3,0},{4,5},{5,6},{6,7},{7,4},{8,9},{9,10},{10,1... | collective-permute-start | bytes 1179656 | tf_op jit(solution)/shard_map/while/body/eval_jaxpr/ppermute | solution.py:16
  487.7 10.9 %collective-permute-start = (bf16[1,256,768]{1,2,0:T(8,128)(2,1)S(1)}, bf16[1,256,768]{1,2,0:T(8,128)(2,1)}, u32[]{:S(2)}, u32[]{:S(2)}) collective-permute-start(bf16[1,256,768]{1,2,0:T(8,128)(2,1)S(1)} %copy.106), channel_id=1, source_target_pairs={{0,1},{1,2},{2,3},{4,5},{5,6},{6,7},{8,9},{9,10},{10,11},{12,13},{... | collective-permute-start | bytes 1179656 | tf_op jit(solution)/shard_map/while/body/eval_jaxpr/ppermute | solution.py:22
  490.4 8.3 collective-permute-start.1
  507.2 181.7 %reduce-scatter.18.cloned.1.call-start = ((), (), s32[]{:S(2)}) async-start(), calls=%async_computation.13 | async-start | bytes 5308416 | tf_op jit(solution)/shard_map/reduce_scatter | solution.py:286
  512.7 274.8 %reduce-scatter.20.cloned.1.call-start = ((), (), s32[]{:S(2)}) async-start(), calls=%async_computation.14 | async-start | bytes 5308416 | tf_op jit(solution)/shard_map/reduce_scatter | solution.py:289
  518.5 355.8 %reduce-scatter.22.cloned.1.call-start = ((), (), s32[]{:S(2)}) async-start(), calls=%async_computation.17 | async-start | bytes 221184
  523.6 266.5 %copy-start.5 = (f32[256,768]{1,0:T(8,128)S(1)}, f32[256,768]{1,0:T(8,128)}, u32[]{:S(2)}) copy-start(f32[256,768]{1,0:T(8,128)} %copy-done.4) | copy-start | bytes 2359300
  523.6 266.5 %copy-start.9 = (f32[256,768]{1,0:T(8,128)S(1)}, f32[256,768]{1,0:T(8,128)}, u32[]{:S(2)}) copy-start(f32[256,768]{1,0:T(8,128)} %copy-done.8) | copy-start | bytes 2359300
  530.1 304.4 %copy-start.41 = (bf16[3072]{0:T(1024)(128)(2,1)S(1)}, bf16[3072]{0:T(1024)(128)(2,1)}, u32[]{:S(2)}) copy-start(bf16[3072]{0:T(1024)(128)(2,1)} %get-tuple-element.569) | copy-start | bytes 18436
  530.1 342.6 %copy-start.21 = (f32[256,768]{1,0:T(8,128)S(1)}, f32[256,768]{1,0:T(8,128)}, u32[]{:S(2)}) copy-start(f32[256,768]{1,0:T(8,128)} %get-tuple-element.599) | copy-start | bytes 2359300
  530.1 386.0 %reduce-scatter.24.cloned.1.call-start = ((), (), s32[]{:S(2)}) async-start(), calls=%async_computation.18 | async-start | bytes 221184
  538.2 441.3 %reduce-scatter.26.cloned.1.call-start = ((), (), s32[]{:S(2)}) async-start(), calls=%async_computation.19 | async-start | bytes 221184
  541.2 486.4 %all-reduce.9.cloned.1.call-start = ((), (), s32[]{:S(2)}) async-start(), calls=%async_computation.20 | async-start | bytes 3538944 | tf_op jit(solution)/shard_map/psum | solution.py:312
  (57 other events, 345.3 us)
Sparse Core Ops, SparseCore 0:
  10.2 67.9 all-gather.14
  82.5 18.1 all-gather.22
  102.9 19.6 all-gather.24
  124.6 41.1 all-gather.16
  167.8 78.6 all-gather.18
  248.5 78.0 all-gather.20
  353.4 62.2 reduce-scatter.15
  507.4 82.7 reduce-scatter.13
  593.8 95.1 reduce-scatter.17
  692.5 94.9 reduce-scatter.19
  791.4 60.8 reduce-scatter.21
  856.0 60.0 reduce-scatter.23
  919.4 60.0 reduce-scatter.25
  982.0 45.6 all-reduce.8
where the time goes:
time: 1050 us; the launch traced here: 1040 us
  waiting for transfers between devices  522 us (50%)
  blocking collectives  218 us (21%)
  other arithmetic  88.9 us (8%)
  matrix products  73 us (7%)
  starting transfers between devices  66.2 us (6%)
  local copies, waits for them, and re-layouts  54.6 us (5%)
  between operations  19.5 us (2%)
    unnamed x17, waiting for transfers between devices  106 us
    reduce_scatter x1, waiting for transfers between devices, shards(): lax.psum_scatter(up_grad.astype(jnp.bfloat16), 'dp', scatter_dimension=0,...  98.8 us
    reduce_scatter x1, waiting for transfers between devices, shards(): lax.psum_scatter(down_grad.astype(jnp.bfloat16), 'dp', scatter_dimension=...  98.5 us
    all_gather x1, waiting for transfers between devices, shards(): lax.all_gather(w_down, 'dp', axis=0, tiled=True)  67.6 us
    reduce_scatter x1, waiting for transfers between devices, shards(): lax.psum_scatter(qkv_grad.astype(jnp.bfloat16), 'dp', scatter_dimension=0...  48.6 us
    ppermute x8, starting transfers between devices, passed_along(): return lax.ppermute(value, axis, pairs)  46.1 us
    psum x1, blocking collectives, shards(): lax.psum((0.5 * jnp.sum(error_rows * error_rows), jnp.sum(valid_mask)), (...  40.5 us
    psum x1, waiting for transfers between devices, shards(): lax.psum(shares[0].astype(jnp.bfloat16), 'ctx').astype(jnp.float32)  38.1 us
  transfers between devices with their start and end apart: 30, of which 9 were waited for; matrix products, arithmetic and copies ran while one was open for 17% of the time, Pallas kernels for 0%

commit v1 on v0

--- a/solution.py
+++ b/solution.py
@@ -309,7 +309,7 @@
         ).astype(jnp.float32),
     )
     summed = (
-        lax.psum(shares[0].astype(jnp.bfloat16), "ctx").astype(jnp.float32),
+        jnp.sum(lax.all_gather(shares[0].astype(jnp.bfloat16), "ctx"), axis=0).astype(jnp.float32),
         lax.psum(shares[1].astype(jnp.bfloat16), "ctx").astype(jnp.float32),
         lax.psum(shares[2].astype(jnp.bfloat16), "ctx").astype(jnp.float32),
         lax.psum(shares[3].astype(jnp.bfloat16), "ctx").astype(jnp.float32),

time: 1050 us -> 1130 us (1.076)
  waiting for transfers between devices: 522 us -> 599 us
    reduce_scatter x1, waiting for transfers between devices: 0.02 us -> 65.6 us  [shards(): lax.psum_scatter(out_grad.astype(jnp.bfloat16), 'dp', scatter_dimension=0...]
    unnamed x17 -> x18, waiting for transfers between devices: 106 us -> 108 us
  transfers between devices with their start and end apart: 30 -> 31, of which waited for: 9 -> 11; matrix products, arithmetic and copies ran while one was open for 17% -> 11% of each run, Pallas kernels for 0% -> 0%
where the time goes in v1:
time: 1130 us; the launch traced here: 1120 us
  waiting for transfers between devices  599 us (53%)
  blocking collectives  219 us (19%)
  other arithmetic  90.5 us (8%)
  matrix products  72.7 us (6%)
  starting transfers between devices  66.3 us (6%)
  local copies, waits for them, and re-layouts  54.9 us (5%)
  between operations  19.4 us (2%)
    unnamed x18, waiting for transfers between devices  108 us
    reduce_scatter x1, waiting for transfers between devices, shards(): lax.psum_scatter(down_grad.astype(jnp.bfloat16), 'dp', scatter_dimension=...  98.5 us
    reduce_scatter x1, waiting for transfers between devices, shards(): lax.psum_scatter(up_grad.astype(jnp.bfloat16), 'dp', scatter_dimension=0,...  98.5 us
    all_gather x1, waiting for transfers between devices, shards(): lax.all_gather(w_down, 'dp', axis=0, tiled=True)  67.3 us
    reduce_scatter x1, waiting for transfers between devices, shards(): lax.psum_scatter(out_grad.astype(jnp.bfloat16), 'dp', scatter_dimension=0...  65.6 us
    ppermute x8, starting transfers between devices, passed_along(): return lax.ppermute(value, axis, pairs)  46.2 us
    reduce_scatter x1, waiting for transfers between devices, shards(): lax.psum_scatter(qkv_grad.astype(jnp.bfloat16), 'dp', scatter_dimension=0...  45.7 us
    psum x1, blocking collectives, shards(): lax.psum((0.5 * jnp.sum(error_rows * error_rows), jnp.sum(valid_mask)), (...  40.6 us
  transfers between devices with their start and end apart: 31, of which 11 were waited for; matrix products, arithmetic and copies ran while one was open for 11% of the time, Pallas kernels for 0%

profile of v1, /device:TPU:0, one launch (start us, length us, event | category | flops | bytes accessed | tf_op | source)
XLA Modules:
  0.0 1121.2 jit_solution(5382936814092778545)
XLA Ops:
  8.0 22.6 %all-gather.4 = bf16[8,96,3]{1,2,0:T(4,128)(2,1)S(1)} all-gather(bf16[1,96,3]{1,2,0:T(4,128)(2,1)} %bitcast.187), channel_id=1, replica_groups=mesh['dp'=8,'ctx'=4] {'dp'}, dimensions={0}, use_global_device_ids=true | all-gather | bytes 5184 | tf_op jit(solution)/shard_map/all_gather | solution.py:141
  30.7 16.6 %all-gather.3 = bf16[8,96,3]{1,2,0:T(4,128)(2,1)S(1)} all-gather(bf16[1,96,3]{1,2,0:T(4,128)(2,1)} %bitcast.188), channel_id=1, replica_groups=mesh['dp'=8,'ctx'=4] {'dp'}, dimensions={0}, use_global_device_ids=true | all-gather | bytes 5184 | tf_op jit(solution)/shard_map/all_gather | solution.py:140
  49.9 28.3 %all-gather.17.cloned.1.call-done = bf16[768,2304]{1,0:T(8,128)(2,1)} async-done(((bf16[96,2304]{1,0:T(8,128)(2,1)}), bf16[768,2304]{1,0:T(8,128)(2,1)}) %all-gather.17.cloned.1.call-update) | async-done | bytes 3538960 | tf_op jit(solution)/shard_map/all_gather | solution.py:136
  78.2 3.3 fusion.73
  82.5 18.1 %all-gather.5 = bf16[8,96,4]{1,2,0:T(4,128)(2,1)S(1)} all-gather(bf16[1,96,4]{1,2,0:T(4,128)(2,1)S(1)} %bitcast.189), channel_id=1, replica_groups=mesh['dp'=8,'ctx'=4] {'dp'}, dimensions={0}, use_global_device_ids=true | all-gather | bytes 6912 | tf_op jit(solution)/shard_map/all_gather | solution.py:142
  104.1 25.9 %all-gather.6 = bf16[8,1,384]{2,1,0:T(2,128)(2,1)S(1)} all-gather(bf16[1,1,384]{2,1,0:T(2,128)(2,1)S(1)} %reshape.471), channel_id=1, replica_groups=mesh['dp'=8,'ctx'=4] {'dp'}, dimensions={0}, use_global_device_ids=true | all-gather | bytes 6912 | tf_op jit(solution)/shard_map/all_gather | solution.py:145
  130.0 26.1 %all-gather.8 = bf16[8,1,384]{2,1,0:T(2,128)(2,1)S(1)} all-gather(bf16[1,1,384]{2,1,0:T(2,128)(2,1)S(1)} %reshape.475), channel_id=1, replica_groups=mesh['dp'=8,'ctx'=4] {'dp'}, dimensions={0}, use_global_device_ids=true | all-gather | bytes 6912 | tf_op jit(solution)/shard_map/all_gather | solution.py:144
  156.1 26.3 %all-gather.7 = bf16[8,1,384]{2,1,0:T(2,128)(2,1)S(1)} all-gather(bf16[1,1,384]{2,1,0:T(2,128)(2,1)S(1)} %reshape.473), channel_id=1, replica_groups=mesh['dp'=8,'ctx'=4] {'dp'}, dimensions={0}, use_global_device_ids=true | all-gather | bytes 6912 | tf_op jit(solution)/shard_map/all_gather | solution.py:143
  185.3 20.6 %conditional.2 = (f32[1,12,256]{2,1,0:T(8,128)}, f32[1,12,256]{2,1,0:T(8,128)}, f32[1,256,12,64]{1,3,2,0:T(8,128)S(1)}, f32[1,12,256]{2,1,0:T(8,128)}) conditional(s32[]{:T(128)} %convert_element_type.249, () %tuple.48, (s32[256]{0:T(256)S(1)}, s32[1]{0:T(128)}, bf16[1,256,12,64]{1,3,2,0:T(8,128)(2,1)}, bf16[1,1024,768]{2,1,0:T(8,128)(2,1)}, ...), branch_computations={%region_2.0_spmd, %region_3.6_spmd} | conditional | flops 840431616 | bytes 106151000 | solution.py:182
  188.0 3.3 fusion.2
  191.9 4.1 fusion.4
  197.7 6.8 fusion.8
  210.5 36.0 %all-gather.21.cloned.1.call-done = bf16[768,3072]{1,0:T(8,128)(2,1)} async-done(((bf16[96,3072]{1,0:T(8,128)(2,1)}), bf16[768,3072]{1,0:T(8,128)(2,1)}) %all-gather.21.cloned.1.call-update) | async-done | bytes 4718608 | tf_op jit(solution)/shard_map/all_gather | solution.py:138
  246.5 12.3 %fusion.85 = (f32[256]{0:T(256)S(1)}, f32[256,3072]{1,0:T(8,128)S(1)}, f32[256,3072]{1,0:T(8,128)}, f32[256,3072]{1,0:T(8,128)}) fusion(f32[3072]{0:T(1024)S(1)} %bitcast.186, bf16[768,3072]{1,0:T(8,128)(2,1)} %all-gather.21.cloned.1.call-done, f32[256,768]{1,0:T(8,128)} %copy-done.6, f32[768]{0:T(1024)S(1)} %get-tuple-element.521, ...), kind=kOutput, calls=%fused_computation.178 | convolution fusion | flops 1260846848 | bytes 14963712 | tf_op jit(solution)/shard_map/dot_general | solution.py:199
  259.3 67.3 %all-gather.23.cloned.1.call-done = bf16[3072,768]{1,0:T(8,128)(2,1)} async-done(((bf16[384,768]{1,0:T(8,128)(2,1)}), bf16[3072,768]{1,0:T(8,128)(2,1)}) %all-gather.23.cloned.1.call-update) | async-done | bytes 4718608 | tf_op jit(solution)/shard_map/all_gather | solution.py:139
  326.6 5.8 convert_reduce_fusion.2
  337.5 3.2 fusion.78
  351.8 144.2 %while.24 = (s32[]{:T(128)}, bf16[1,256,768]{1,2,0:T(8,128)(2,1)}, bf16[1,256,768]{1,2,0:T(8,128)(2,1)}, f32[1,256,768]{1,2,0:T(8,128)}, f32[1,256,768]{1,2,0:T(...) while((s32[]{:T(128)}, bf16[1,256,768]{1,2,0:T(8,128)(2,1)}, ...), condition=%wide.region_25.26_spmd.clone, body=%wide.region_22.25_spmd.clone.sunk | while | flops 513672192 | bytes 48655496 | solution.py:263
  355.3 14.6 %conditional.5 = (f32[1,256,12,64]{1,3,2,0:T(8,128)}, f32[1,256,768]{1,2,0:T(8,128)}, f32[1,256,768]{1,2,0:T(8,128)}) conditional(s32[]{:T(128)} %convert_element_type.409, () %tuple.115, (s32[]{:T(128)}, s32[]{:T(128)}, s32[1]{0:T(128)}, bf16[1,256,12,64]{1,3,2,0:T(8,128)(2,1)}, bf16[1,256,768]{1,2,0:T(8,128)(2,1)S(1)}, ...), branch_computations={%region_23.23_spmd, %region_24.24_spmd} | conditional | flops 511706112 | bytes 32138860 | solution.py:251
  355.3 3.3 fusion.28
  360.0 3.5 multiply_convert_fusion
  367.3 2.7 fusion.18
  375.5 2.7 collective-permute-start
  390.1 2.8 conditional.5
  395.1 16.3 %collective-permute-start.2 = (bf16[1,256,768]{1,2,0:T(8,128)(2,1)}, bf16[1,256,768]{1,2,0:T(8,128)(2,1)}, u32[]{:S(2)}, u32[]{:S(2)}) collective-permute-start(bf16[1,256,768]{1,2,0:T(8,128)(2,1)} %fusion.110), channel_id=1, source_target_pairs={{0,1},{1,2},{2,3},{3,0},{4,5},{5,6},{6,7},{7,4},{8,9},{9,10},{10,1... | collective-permute-start | bytes 1179656 | tf_op jit(solution)/shard_map/while/body/eval_jaxpr/ppermute | solution.py:16
  416.1 2.7 collective-permute-start
  430.4 2.8 conditional.5
  435.4 4.5 collective-permute-start.2
  442.2 14.3 %collective-permute-start.3 = (bf16[1,256,768]{1,2,0:T(8,128)(2,1)}, bf16[1,256,768]{1,2,0:T(8,128)(2,1)}, u32[]{:S(2)}, u32[]{:S(2)}) collective-permute-start(bf16[1,256,768]{1,2,0:T(8,128)(2,1)} %fusion.111), channel_id=1, source_target_pairs={{0,1},{1,2},{2,3},{3,0},{4,5},{5,6},{6,7},{7,4},{8,9},{9,10},{10,1... | collective-permute-start | bytes 1179656 | tf_op jit(solution)/shard_map/while/body/eval_jaxpr/ppermute | solution.py:16
  456.5 2.7 collective-permute-start
  470.8 2.8 conditional.5
  475.8 4.5 collective-permute-start.2
  501.4 3.1 convolution_convert_fusion.2
  504.6 2.9 convolution_convert_fusion.3
  507.6 5.4 convolution_convert_fusion.1
  513.7 5.1 convolution_convert_fusion
  520.0 3.9 fusion.77
  541.7 45.7 %reduce-scatter.14.cloned.1.call-done = bf16[96,2304]{1,0:T(8,128)(2,1)} async-done(((bf16[768,2304]{1,0:T(8,128)(2,1)}), bf16[96,2304]{1,0:T(8,128)(2,1)}) %reduce-scatter.14.cloned.1.call-update) | async-done | bytes 442384 | tf_op jit(solution)/shard_map/reduce_scatter | solution.py:280
  589.3 65.6 %reduce-scatter.16.cloned.1.call-done = bf16[96,768]{1,0:T(8,128)(2,1)} async-done(((bf16[768,768]{1,0:T(8,128)(2,1)}), bf16[96,768]{1,0:T(8,128)(2,1)}) %reduce-scatter.16.cloned.1.call-update) | async-done | bytes 147472 | tf_op jit(solution)/shard_map/reduce_scatter | solution.py:283
  654.9 98.5 %reduce-scatter.18.cloned.1.call-done = bf16[96,3072]{1,0:T(8,128)(2,1)} async-done(((bf16[768,3072]{1,0:T(8,128)(2,1)}), bf16[96,3072]{1,0:T(8,128)(2,1)}) %reduce-scatter.18.cloned.1.call-update) | async-done | bytes 589840 | tf_op jit(solution)/shard_map/reduce_scatter | solution.py:286
  753.4 98.5 %reduce-scatter.20.cloned.1.call-done = bf16[384,768]{1,0:T(8,128)(2,1)} async-done(((bf16[3072,768]{1,0:T(8,128)(2,1)}), bf16[384,768]{1,0:T(8,128)(2,1)}) %reduce-scatter.20.cloned.1.call-update) | async-done | bytes 589840 | tf_op jit(solution)/shard_map/reduce_scatter | solution.py:289
  856.5 40.6 %all-reduce.3 = (f32[]{:T(128)}, f32[]{:T(128)}) all-reduce(f32[]{:T(128)S(6)} %mul.346, f32[]{:T(128)} %fusion.71), channel_id=1, replica_groups=mesh['dp'=8,'ctx'=4] {'dp','ctx'}, use_global_device_ids=true, to_apply=%region_13.14 | all-reduce | flops 2 | bytes 16 | tf_op jit(solution)/shard_map/psum | solution.py:209
  897.0 36.7 %all-reduce.4 = (bf16[3072]{0:T(1024)(128)(2,1)S(1)}, bf16[3072]{0:T(1024)(128)(2,1)S(1)}, bf16[3072]{0:T(1024)(128)(2,1)S(1)}) all-reduce(bf16[3072]{0:T(1024)(128)(2,1)} %get-tuple-element.504, bf16[3072]{0:T(1024)(128)(2,1)} %get-tuple-element.506, bf16[3072]{0:T(1024)(128)(2,1)S(1)} %copy-done.38), channel_id=12, replica_groups=mesh['dp'=8,'ctx'=4] {'dp'}, use_global_device_ids=true, to_apply=%region_53.54.clone | all-reduce | flops 9216 | bytes 36864
  937.6 43.0 %reduce-scatter.24.cloned.1.call-done = bf16[96,3]{1,0:T(8,128)(2,1)} async-done(((bf16[768,3]{1,0:T(8,128)(2,1)}), bf16[96,3]{1,0:T(8,128)(2,1)}) %reduce-scatter.24.cloned.1.call-update) | async-done | bytes 592
  981.4 62.6 %reduce-scatter.26.cloned.1.call-done = bf16[96,4]{1,0:T(8,128)(2,1)} async-done(((bf16[768,4]{1,0:T(8,128)(2,1)}), bf16[96,4]{1,0:T(8,128)(2,1)}) %reduce-scatter.26.cloned.1.call-update) | async-done | bytes 784
  1044.8 5.7 all-reduce.5
  1054.0 11.2 all-gather.29.cloned.1.call-done
  1067.9 39.4 %all-reduce.9.cloned.1.call-done = (bf16[96,768]{1,0:T(8,128)(2,1)}, bf16[96,3072]{1,0:T(8,128)(2,1)}, bf16[384,768]{1,0:T(8,128)(2,1)}) async-done(((bf16[96,768]{1,0:T(8,128)(2,1)}, bf16[96,3072]{1,0:T(8,128)(2,1)}, bf16[384,768]{1,0:T(8,128)(2,1)}), (bf16[96,768]{1,0:T(8,128)(2,1)}, bf16[96,3072]{1,0:T(8,128)(2,1)}, bf16[384,768]{1,0:T(8,128)(2,1)})) %all-reduce.9.cloned.1.call-update) | async-done | bytes 1327120 | tf_op jit(solution)/shard_map/psum | solution.py:313
  (346 shorter events, 170.6 us)
Async XLA Ops:
  7.2 71.0 %all-gather.17.cloned.1.call-start = ((), (), s32[]{:S(2)}) async-start(), calls=%async_computation.7 | async-start | bytes 3981312 | tf_op jit(solution)/shard_map/all_gather | solution.py:136
  7.9 177.4 %all-gather.25.cloned.1.call-start = ((), (), s32[]{:S(2)}) async-start(), calls=%async_computation.15 | async-start | bytes 1966080 | tf_op jit(solution)/shard_map/all_gather | solution.py:178
  47.4 159.9 %copy-start.43 = (f32[768]{0:T(1024)}, f32[768]{0:T(1024)S(1)}, u32[]{:S(2)}) copy-start(f32[768]{0:T(1024)S(1)} %get-tuple-element.522) | copy-start | bytes 9220
  47.4 199.0 %copy-start.31 = (f32[768]{0:T(1024)}, f32[768]{0:T(1024)S(1)}, u32[]{:S(2)}) copy-start(f32[768]{0:T(1024)S(1)} %get-tuple-element.521) | copy-start | bytes 9220
  47.4 299.6 %copy-start.32 = (f32[768]{0:T(1024)}, f32[768]{0:T(1024)S(1)}, u32[]{:S(2)}) copy-start(f32[768]{0:T(1024)S(1)} %get-tuple-element.604) | copy-start | bytes 9220
  81.6 74.5 %copy-start.62 = (bf16[384]{0:T(512)(128)(2,1)S(1)}, bf16[384]{0:T(512)(128)(2,1)}, u32[]{:S(2)}) copy-start(bf16[384]{0:T(512)(128)(2,1)} %param.29) | copy-start | bytes 2308
  82.4 102.9 %all-gather.27.cloned.1.call-start = ((), (), s32[]{:S(2)}) async-start(), calls=%async_computation.16 | async-start | bytes 1966080 | tf_op jit(solution)/shard_map/all_gather | solution.py:179
  101.6 82.9 %copy-start.16 = (bf16[256,768]{1,0:T(8,128)(2,1)S(1)}, bf16[256,768]{1,0:T(8,128)(2,1)}, u32[]{:S(2)}) copy-start(bf16[256,768]{1,0:T(8,128)(2,1)} %get-tuple-element.591) | copy-start | bytes 1179652
  101.6 105.8 %all-gather.19.cloned.1.call-start = ((), (), s32[]{:S(2)}) async-start(), calls=%async_computation.8 | async-start | bytes 1327104 | tf_op jit(solution)/shard_map/all_gather | solution.py:137
  102.2 144.3 %all-gather.21.cloned.1.call-start = ((), (), s32[]{:S(2)}) async-start(), calls=%async_computation.9 | async-start | bytes 5308416 | tf_op jit(solution)/shard_map/all_gather | solution.py:138
  102.7 223.8 %all-gather.23.cloned.1.call-start = ((), (), s32[]{:S(2)}) async-start(), calls=%async_computation.10 | async-start | bytes 5308416 | tf_op jit(solution)/shard_map/all_gather | solution.py:139
  103.3 484.1 %reduce-scatter.14.cloned.1.call-start = ((), (), s32[]{:S(2)}) async-start(), calls=%async_computation.11 | async-start | bytes 3981312 | tf_op jit(solution)/shard_map/reduce_scatter | solution.py:280
  156.1 170.4 %copy-start.28 = (f32[8,1,384]{2,1,0:T(1,128)}, f32[8,1,384]{2,1,0:T(1,128)S(1)}, u32[]{:S(2)}) copy-start(f32[8,1,384]{2,1,0:T(1,128)S(1)} %convert_element_type.302) | copy-start | bytes 36868
  182.5 144.0 %copy-start.56 = (f32[256]{0:T(256)}, f32[256]{0:T(256)S(1)}, u32[]{:S(2)}) copy-start(f32[256]{0:T(256)S(1)} %compare_convert_fusion) | copy-start | bytes 3076
  207.1 139.9 %copy-start.42 = (f32[256]{0:T(256)}, f32[256]{0:T(256)S(1)}, u32[]{:S(2)}) copy-start(f32[256]{0:T(256)S(1)} %broadcast_multiply_fusion.2) | copy-start | bytes 3076
  207.3 139.7 %copy-start.51 = (f32[256]{0:T(256)}, f32[256]{0:T(256)S(1)}, u32[]{:S(2)}) copy-start(f32[256]{0:T(256)S(1)} %fusion.63) | copy-start | bytes 3076
  209.3 134.8 %copy-start.37 = (f32[256]{0:T(256)}, f32[256]{0:T(256)S(1)}, u32[]{:S(2)}) copy-start(f32[256]{0:T(256)S(1)} %broadcast_multiply_fusion.1) | copy-start | bytes 3076
  210.4 133.7 %copy-start.45 = (f32[256]{0:T(256)}, f32[256]{0:T(256)S(1)}, u32[]{:S(2)}) copy-start(f32[256]{0:T(256)S(1)} %fusion.64) | copy-start | bytes 3076
  258.8 77.7 %copy-start.29 = (f32[256]{0:T(256)}, f32[256]{0:T(256)S(1)}, u32[]{:S(2)}) copy-start(f32[256]{0:T(256)S(1)} %broadcast_multiply_fusion) | copy-start | bytes 3076
  259.3 77.2 %copy-start.36 = (f32[256]{0:T(256)}, f32[256]{0:T(256)S(1)}, u32[]{:S(2)}) copy-start(f32[256]{0:T(256)S(1)} %fusion.65) | copy-start | bytes 3076
  371.9 10.9 collective-permute-start.2
  373.9 10.9 collective-permute-start.3
  375.5 11.2 %collective-permute-start = (bf16[1,256,768]{1,2,0:T(8,128)(2,1)S(1)}, bf16[1,256,768]{1,2,0:T(8,128)(2,1)}, u32[]{:S(2)}, u32[]{:S(2)}) collective-permute-start(bf16[1,256,768]{1,2,0:T(8,128)(2,1)S(1)} %copy.106), channel_id=1, source_target_pairs={{0,1},{1,2},{2,3},{4,5},{5,6},{6,7},{8,9},{9,10},{10,11},{12,13},{... | collective-permute-start | bytes 1179656 | tf_op jit(solution)/shard_map/while/body/eval_jaxpr/ppermute | solution.py:22
  378.2 8.6 collective-permute-start.1
  395.1 28.0 %collective-permute-start.2 = (bf16[1,256,768]{1,2,0:T(8,128)(2,1)}, bf16[1,256,768]{1,2,0:T(8,128)(2,1)}, u32[]{:S(2)}, u32[]{:S(2)}) collective-permute-start(bf16[1,256,768]{1,2,0:T(8,128)(2,1)} %fusion.110), channel_id=1, source_target_pairs={{0,1},{1,2},{2,3},{3,0},{4,5},{5,6},{6,7},{7,4},{8,9},{9,10},{10,1... | collective-permute-start | bytes 1179656 | tf_op jit(solution)/shard_map/while/body/eval_jaxpr/ppermute | solution.py:16
  413.6 11.5 %collective-permute-start.3 = (bf16[1,256,768]{1,2,0:T(8,128)(2,1)}, bf16[1,256,768]{1,2,0:T(8,128)(2,1)}, u32[]{:S(2)}, u32[]{:S(2)}) collective-permute-start(bf16[1,256,768]{1,2,0:T(8,128)(2,1)} %fusion.111), channel_id=1, source_target_pairs={{0,1},{1,2},{2,3},{3,0},{4,5},{5,6},{6,7},{7,4},{8,9},{9,10},{10,1... | collective-permute-start | bytes 1179656 | tf_op jit(solution)/shard_map/while/body/eval_jaxpr/ppermute | solution.py:16
  416.1 10.9 collective-permute-start
  418.8 8.3 collective-permute-start.1
  435.4 28.1 %collective-permute-start.2 = (bf16[1,256,768]{1,2,0:T(8,128)(2,1)}, bf16[1,256,768]{1,2,0:T(8,128)(2,1)}, u32[]{:S(2)}, u32[]{:S(2)}) collective-permute-start(bf16[1,256,768]{1,2,0:T(8,128)(2,1)} %fusion.110), channel_id=1, source_target_pairs={{0,1},{1,2},{2,3},{3,0},{4,5},{5,6},{6,7},{7,4},{8,9},{9,10},{10,1... | collective-permute-start | bytes 1179656 | tf_op jit(solution)/shard_map/while/body/eval_jaxpr/ppermute | solution.py:16
  442.2 23.3 %collective-permute-start.3 = (bf16[1,256,768]{1,2,0:T(8,128)(2,1)}, bf16[1,256,768]{1,2,0:T(8,128)(2,1)}, u32[]{:S(2)}, u32[]{:S(2)}) collective-permute-start(bf16[1,256,768]{1,2,0:T(8,128)(2,1)} %fusion.111), channel_id=1, source_target_pairs={{0,1},{1,2},{2,3},{3,0},{4,5},{5,6},{6,7},{7,4},{8,9},{9,10},{10,1... | collective-permute-start | bytes 1179656 | tf_op jit(solution)/shard_map/while/body/eval_jaxpr/ppermute | solution.py:16
  456.5 10.9 collective-permute-start
  459.2 8.3 collective-permute-start.1
  475.8 16.3 %collective-permute-start.2 = (bf16[1,256,768]{1,2,0:T(8,128)(2,1)}, bf16[1,256,768]{1,2,0:T(8,128)(2,1)}, u32[]{:S(2)}, u32[]{:S(2)}) collective-permute-start(bf16[1,256,768]{1,2,0:T(8,128)(2,1)} %fusion.110), channel_id=1, source_target_pairs={{0,1},{1,2},{2,3},{3,0},{4,5},{5,6},{6,7},{7,4},{8,9},{9,10},{10,1... | collective-permute-start | bytes 1179656 | tf_op jit(solution)/shard_map/while/body/eval_jaxpr/ppermute | solution.py:16
  482.6 11.5 %collective-permute-start.3 = (bf16[1,256,768]{1,2,0:T(8,128)(2,1)}, bf16[1,256,768]{1,2,0:T(8,128)(2,1)}, u32[]{:S(2)}, u32[]{:S(2)}) collective-permute-start(bf16[1,256,768]{1,2,0:T(8,128)(2,1)} %fusion.111), channel_id=1, source_target_pairs={{0,1},{1,2},{2,3},{3,0},{4,5},{5,6},{6,7},{7,4},{8,9},{9,10},{10,1... | collective-permute-start | bytes 1179656 | tf_op jit(solution)/shard_map/while/body/eval_jaxpr/ppermute | solution.py:16
  485.1 10.9 collective-permute-start
  487.7 8.3 collective-permute-start.1
  504.6 150.3 %reduce-scatter.16.cloned.1.call-start = ((), (), s32[]{:S(2)}) async-start(), calls=%async_computation.12 | async-start | bytes 1327104 | tf_op jit(solution)/shard_map/reduce_scatter | solution.py:283
  507.6 245.8 %reduce-scatter.18.cloned.1.call-start = ((), (), s32[]{:S(2)}) async-start(), calls=%async_computation.13 | async-start | bytes 5308416 | tf_op jit(solution)/shard_map/reduce_scatter | solution.py:286
  513.0 338.9 %reduce-scatter.20.cloned.1.call-start = ((), (), s32[]{:S(2)}) async-start(), calls=%async_computation.14 | async-start | bytes 5308416 | tf_op jit(solution)/shard_map/reduce_scatter | solution.py:289
  518.8 418.0 %reduce-scatter.22.cloned.1.call-start = ((), (), s32[]{:S(2)}) async-start(), calls=%async_computation.18 | async-start | bytes 221184
  523.9 328.7 %copy-start.5 = (f32[256,768]{1,0:T(8,128)S(1)}, f32[256,768]{1,0:T(8,128)}, u32[]{:S(2)}) copy-start(f32[256,768]{1,0:T(8,128)} %copy-done.4) | copy-start | bytes 2359300
  523.9 328.7 %copy-start.9 = (f32[256,768]{1,0:T(8,128)S(1)}, f32[256,768]{1,0:T(8,128)}, u32[]{:S(2)}) copy-start(f32[256,768]{1,0:T(8,128)} %copy-done.8) | copy-start | bytes 2359300
  530.5 366.6 %copy-start.38 = (bf16[3072]{0:T(1024)(128)(2,1)S(1)}, bf16[3072]{0:T(1024)(128)(2,1)}, u32[]{:S(2)}) copy-start(bf16[3072]{0:T(1024)(128)(2,1)} %get-tuple-element.568) | copy-start | bytes 18436
  530.5 404.8 %copy-start.21 = (f32[256,768]{1,0:T(8,128)S(1)}, f32[256,768]{1,0:T(8,128)}, u32[]{:S(2)}) copy-start(f32[256,768]{1,0:T(8,128)} %get-tuple-element.598) | copy-start | bytes 2359300
  530.5 450.1 %reduce-scatter.24.cloned.1.call-start = ((), (), s32[]{:S(2)}) async-start(), calls=%async_computation.19 | async-start | bytes 221184
  538.8 505.2 %reduce-scatter.26.cloned.1.call-start = ((), (), s32[]{:S(2)}) async-start(), calls=%async_computation.20 | async-start | bytes 221184
  541.7 523.5 %all-gather.29.cloned.1.call-start = ((), (), s32[]{:S(2)}) async-start(), calls=%async_computation.17 | async-start | bytes 2211840 | tf_op jit(solution)/shard_map/all_gather | solution.py:312
  587.4 520.0 %all-reduce.9.cloned.1.call-start = ((), (), s32[]{:S(2)}) async-start(), calls=%async_computation.21 | async-start | bytes 2654208 | tf_op jit(solution)/shard_map/psum | solution.py:313
  (49 other events, 412.1 us)
Sparse Core Ops, SparseCore 0:
  10.2 67.9 all-gather.16
  82.5 18.1 all-gather.24
  102.9 19.6 all-gather.26
  124.6 41.1 all-gather.18
  167.8 78.6 all-gather.20
  248.5 78.0 all-gather.22
  504.7 82.6 reduce-scatter.13
  591.3 63.5 reduce-scatter.15
  658.6 94.7 reduce-scatter.17
  756.9 94.9 reduce-scatter.19
  855.7 60.8 reduce-scatter.21
  920.3 60.1 reduce-scatter.23
  983.8 60.1 reduce-scatter.25
  1045.4 19.7 all-gather.28
  1067.6 39.7 all-reduce.8
